TPU v7x, 32 devices: a whole 2x2x4 slice. The times are simulated.
32 devices in a mesh: layer: 2 (over y), row: 4 (over z), col: 4 (over x, core).
Axes of the slice: x: 2, y: 2, z: 4, core: 2. Of those that a mesh axis runs over, the one named last changes fastest.
Arguments:
- right_side: float32 [16, 4, 64, 128], P(None, 'row', 'layer'), may hold values from -6 to 6
- below: float32 [2, 16, 4, 64, 128], P('layer', None, 'row'), may hold values from -4 to 4
- diag_inverse: float32 [4, 4, 4, 4, 4, 128, 128], P(None, None, 'row', None, 'col'), as said below
- factor_blocks: float32 [4, 4, 4, 128, 128], P('row', 'col'), may hold values from -0.125 to 0.125
- block_row: int32 [4, 4, 4], P('row', 'col'), may hold values from 16 to 63, as said below
- block_col: int32 [4, 4, 4], P('row', 'col'), may hold values from 0 to 47, as said below
Outputs:
- solution: float32 [16, 4, 64, 128], P(None, 'row', 'layer')
Inputs may be any that keep to these rules, and one draw needn't show every extreme that they name: block_row[r, c, n] % 4 == r. block_col[r, c, n] % 4 == c, and block_col[r, c, n] // 16 < block_row[r, c, n] // 16. `diag_inverse`: blocks with k < m are zero and blocks with k == m are lower triangular; the diagonal entries of the diagonal blocks lie in 0.5 to 1.5; the other entries below the diagonal are of mean zero with a spread of about 0.5 / sqrt(128) inside the diagonal blocks and 0.5 / sqrt(2048) in the blocks with k > m, not bounded.
All inputs are finite; a program needn't handle non-finite values.
Results may differ from a plain program's by a relative error of at most 0.0001.
Values sent between devices are 32-bit elements; how exact they have to be, the bound alone decides.
A program may use at most 64 MiB of HBM per device.

v0:
```python
import jax
import jax.numpy as jnp
from jax import lax
from jax.sharding import PartitionSpec as P

BLK = 128
NB = 16
STEPS = 4


def body(right_side, below, diag_inverse, factor_blocks, block_row, block_col):
    rows_count = lax.axis_size("row")
    cols_count = lax.axis_size("col")
    col_self = lax.axis_index("col")
    own_rhs = right_side[:, 0]
    local_rows = own_rhs.shape[0]
    rhs_width = own_rhs.shape[1]
    each_supernode_list = NB // rows_count
    col_width = NB // cols_count
    listed = factor_blocks[0, 0]
    row_index = block_row[0, 0]
    col_index = block_col[0, 0]
    row_onehot = (row_index[:, None] // rows_count == jnp.arange(local_rows)[None, :]).astype(
        jnp.float32
    )
    inverted_diagonal = diag_inverse[:, :, 0, :, 0]
    merged = own_rhs - lax.psum_scatter(below[0, :, 0], "layer", scatter_dimension=1, tiled=True)
    accumulated = jnp.zeros_like(own_rhs)
    solved_pieces = []
    for current_supernode in range(STEPS):
        first_row = current_supernode * each_supernode_list
        last_row = first_row + each_supernode_list
        merged_part = merged[first_row:last_row]
        offset = col_index - current_supernode * NB
        active = ((offset >= 0) & (offset < NB)).astype(jnp.float32)
        summed = lax.psum(accumulated[first_row:last_row], "col")
        target_rows = merged_part - summed
        relayed = lax.all_gather(target_rows[:, None], "row", axis=1, tiled=True).reshape(
            NB, rhs_width, BLK
        )
        local_target_rows = lax.dynamic_index_in_dim(
            relayed.reshape(col_width, cols_count, rhs_width, BLK), col_self, 1, keepdims=False
        )
        partial_solved = jnp.einsum(
            "exnc,xvc->evn",
            inverted_diagonal[current_supernode],
            local_target_rows,
            precision=lax.Precision.HIGHEST,
        )
        solved_own = lax.psum(partial_solved, "col")
        if current_supernode + 1 < STEPS:
            solved_all = lax.all_gather(solved_own[:, None], "row", axis=1, tiled=True).reshape(
                NB, rhs_width, BLK
            )
            chosen = jnp.take(solved_all, jnp.clip(offset, 0, NB - 1), axis=0)
        solved_pieces.append(solved_own)
        if current_supernode + 1 < STEPS:
            products = jnp.einsum("nrb,nab->nra", chosen, listed, precision=lax.Precision.HIGHEST)
            accumulated = accumulated + jnp.einsum(
                "nq,nra->qra",
                row_onehot * active[:, None],
                products,
                precision=lax.Precision.HIGHEST,
            )
    solution = jnp.concatenate(solved_pieces, axis=0)
    return solution[:, None]


def solution(mesh):
    return jax.shard_map(
        body,
        mesh=mesh,
        in_specs=(
            P(None, "row", "layer", None),
            P("layer", None, "row", None, None),
            P(None, None, "row", None, "col", None, None),
            P("row", "col", None, None, None),
            P("row", "col", None),
            P("row", "col", None),
        ),
        out_specs=P(None, "row", "layer", None),
        check_vma=False,
    )
```

profile of v0, /device:TPU:0, one launch (start us, length us, event | category | flops | bytes accessed | tf_op | source)
XLA Modules:
  0.0 379.0 jit_solution(7818879516390627955)
XLA Ops:
  6.5 2.2 copy.56
  10.8 16.2 %reduce-scatter.2.cloned.1.call-done = f32[16,32,128]{2,0,1:T(8,128)} async-done(((f32[16,64,128]{2,0,1:T(8,128)}), f32[16,32,128]{2,0,1:T(8,128)}) %reduce-scatter.2.cloned.1.call-update) | async-done | bytes 262160 | tf_op jit(solution)/shard_map/reduce_scatter | solution.py:27
  27.0 1.2 bitcast_subtract_fusion
  28.2 13.9 %all-gather = f32[4,128,128]{2,0,1:T(4,128)S(1)} all-gather(f32[4,32,128]{2,0,1:T(4,128)S(1)} %slice.55), channel_id=2, replica_groups=mesh['layer'=2,'row'=4,'col'=4] {'row'}, dimensions={1}, use_global_device_ids=true | all-gather | bytes 327680 | tf_op jit(solution)/shard_map/all_gather | solution.py:38
  42.1 2.9 convolution_bitcast_fusion.3
  45.1 32.2 %all-reduce.8.cloned.1.call-done = f32[4,32,128]{2,1,0:T(8,128)} async-done(((f32[4,32,128]{2,1,0:T(8,128)}), f32[4,32,128]{2,1,0:T(8,128)}) %all-reduce.8.cloned.1.call-update) | async-done | bytes 65552 | tf_op jit(solution)/shard_map/psum | solution.py:50
  77.3 14.1 %all-gather.1 = f32[4,128,128]{2,1,0:T(8,128)S(1)} all-gather(f32[4,32,128]{2,1,0:T(8,128)} %all-reduce.8.cloned.1.call-done), channel_id=3, replica_groups=mesh['layer'=2,'row'=4,'col'=4] {'row'}, dimensions={1}, use_global_device_ids=true | all-gather | bytes 327680 | tf_op jit(solution)/shard_map/all_gather | solution.py:52
  93.8 31.8 %all-reduce.10.cloned.1.call-done = f32[4,32,128]{2,0,1:T(4,128)} async-done(((f32[4,32,128]{2,0,1:T(4,128)}), f32[4,32,128]{2,0,1:T(4,128)}) %all-reduce.10.cloned.1.call-update) | async-done | bytes 65552 | tf_op jit(solution)/shard_map/psum | solution.py:36
  125.5 0.9 slice_subtract_fusion.2
  126.4 13.9 %all-gather.2 = f32[4,128,128]{2,0,1:T(4,128)S(1)} all-gather(f32[4,32,128]{2,0,1:T(4,128)S(1)} %slice_subtract_fusion.2), channel_id=4, replica_groups=mesh['layer'=2,'row'=4,'col'=4] {'row'}, dimensions={1}, use_global_device_ids=true | all-gather | bytes 327680 | tf_op jit(solution)/shard_map/all_gather | solution.py:38
  140.3 2.9 convolution_bitcast_fusion.2
  143.3 31.8 %all-reduce.12.cloned.1.call-done = f32[4,32,128]{2,1,0:T(8,128)} async-done(((f32[4,32,128]{2,1,0:T(8,128)}), f32[4,32,128]{2,1,0:T(8,128)}) %all-reduce.12.cloned.1.call-update) | async-done | bytes 65552 | tf_op jit(solution)/shard_map/psum | solution.py:50
  175.0 14.2 %all-gather.3 = f32[4,128,128]{2,1,0:T(8,128)S(1)} all-gather(f32[4,32,128]{2,1,0:T(8,128)} %all-reduce.12.cloned.1.call-done), channel_id=5, replica_groups=mesh['layer'=2,'row'=4,'col'=4] {'row'}, dimensions={1}, use_global_device_ids=true | all-gather | bytes 327680 | tf_op jit(solution)/shard_map/all_gather | solution.py:52
  191.6 31.8 %all-reduce.14.cloned.1.call-done = f32[4,32,128]{2,0,1:T(4,128)} async-done(((f32[4,32,128]{2,0,1:T(4,128)}), f32[4,32,128]{2,0,1:T(4,128)}) %all-reduce.14.cloned.1.call-update) | async-done | bytes 65552 | tf_op jit(solution)/shard_map/psum | solution.py:36
  224.2 13.9 %all-gather.4 = f32[4,128,128]{2,0,1:T(4,128)S(1)} all-gather(f32[4,32,128]{2,0,1:T(4,128)S(1)} %slice_subtract_fusion.1), channel_id=6, replica_groups=mesh['layer'=2,'row'=4,'col'=4] {'row'}, dimensions={1}, use_global_device_ids=true | all-gather | bytes 327680 | tf_op jit(solution)/shard_map/all_gather | solution.py:38
  238.1 2.9 convolution_bitcast_fusion.1
  241.1 31.8 %all-reduce.16.cloned.1.call-done = f32[4,32,128]{2,1,0:T(8,128)} async-done(((f32[4,32,128]{2,1,0:T(8,128)}), f32[4,32,128]{2,1,0:T(8,128)}) %all-reduce.16.cloned.1.call-update) | async-done | bytes 65552 | tf_op jit(solution)/shard_map/psum | solution.py:50
  272.8 14.1 %all-gather.5 = f32[4,128,128]{2,1,0:T(8,128)S(1)} all-gather(f32[4,32,128]{2,1,0:T(8,128)} %all-reduce.16.cloned.1.call-done), channel_id=7, replica_groups=mesh['layer'=2,'row'=4,'col'=4] {'row'}, dimensions={1}, use_global_device_ids=true | all-gather | bytes 327680 | tf_op jit(solution)/shard_map/all_gather | solution.py:52
  289.3 31.8 %all-reduce.18.cloned.1.call-done = f32[4,32,128]{2,0,1:T(4,128)} async-done(((f32[4,32,128]{2,0,1:T(4,128)}), f32[4,32,128]{2,0,1:T(4,128)}) %all-reduce.18.cloned.1.call-update) | async-done | bytes 65552 | tf_op jit(solution)/shard_map/psum | solution.py:36
  321.1 0.9 slice_subtract_fusion
  321.9 13.9 %all-gather.6 = f32[4,128,128]{2,0,1:T(4,128)S(1)} all-gather(f32[4,32,128]{2,0,1:T(4,128)S(1)} %slice_subtract_fusion), channel_id=8, replica_groups=mesh['layer'=2,'row'=4,'col'=4] {'row'}, dimensions={1}, use_global_device_ids=true | all-gather | bytes 327680 | tf_op jit(solution)/shard_map/all_gather | solution.py:38
  335.8 2.9 convolution_bitcast_fusion
  338.7 31.8 %all-reduce.20.cloned.1.call-done = f32[4,32,128]{2,1,0:T(8,128)} async-done(((f32[4,32,128]{2,1,0:T(8,128)}), f32[4,32,128]{2,1,0:T(8,128)}) %all-reduce.20.cloned.1.call-update) | async-done | bytes 65552 | tf_op jit(solution)/shard_map/psum | solution.py:50
  370.5 1.6 maximum_bitcast_fusion
  (46 shorter events, 10.2 us)
Async XLA Ops:
  6.5 85.4 %copy-start = (f32[1,1,4,128,128]{4,3,2,1,0:T(8,128)S(1)}, f32[1,1,4,128,128]{4,3,2,1,0:T(8,128)}, u32[]{:S(2)}) copy-start(f32[1,1,4,128,128]{4,3,2,1,0:T(8,128)} %param.11) | copy-start | bytes 786436
  6.5 20.4 %reduce-scatter.2.cloned.1.call-start = ((), (), s32[]{:S(2)}) async-start(), calls=%async_computation.1 | async-start | bytes 786432 | tf_op jit(solution)/shard_map/reduce_scatter | solution.py:27
  8.7 68.6 %all-reduce.8.cloned.1.call-start = ((), (), s32[]{:S(2)}) async-start(), calls=%async_computation.2 | async-start | bytes 131072 | tf_op jit(solution)/shard_map/psum | solution.py:50
  45.0 80.5 %all-reduce.10.cloned.1.call-start = ((), (), s32[]{:S(2)}) async-start(), calls=%async_computation.3 | async-start | bytes 131072 | tf_op jit(solution)/shard_map/psum | solution.py:36
  93.7 81.3 %all-reduce.12.cloned.1.call-start = ((), (), s32[]{:S(2)}) async-start(), calls=%async_computation.4 | async-start | bytes 131072 | tf_op jit(solution)/shard_map/psum | solution.py:50
  140.3 230.3 %copy-start.1 = (f32[4,32,128]{2,1,0:T(8,128)S(1)}, f32[4,32,128]{2,1,0:T(8,128)}, u32[]{:S(2)}) copy-start(f32[4,32,128]{2,1,0:T(8,128)} %all-reduce.8.cloned.1.call-done) | copy-start | bytes 196612
  143.2 80.2 %all-reduce.14.cloned.1.call-start = ((), (), s32[]{:S(2)}) async-start(), calls=%async_computation.5 | async-start | bytes 131072 | tf_op jit(solution)/shard_map/psum | solution.py:36
  175.0 195.5 %copy-start.2 = (f32[4,32,128]{2,1,0:T(8,128)S(1)}, f32[4,32,128]{2,1,0:T(8,128)}, u32[]{:S(2)}) copy-start(f32[4,32,128]{2,1,0:T(8,128)} %all-reduce.12.cloned.1.call-done) | copy-start | bytes 196612
  191.6 81.3 %all-reduce.16.cloned.1.call-start = ((), (), s32[]{:S(2)}) async-start(), calls=%async_computation.6 | async-start | bytes 131072 | tf_op jit(solution)/shard_map/psum | solution.py:50
  241.0 80.1 %all-reduce.18.cloned.1.call-start = ((), (), s32[]{:S(2)}) async-start(), calls=%async_computation.7 | async-start | bytes 131072 | tf_op jit(solution)/shard_map/psum | solution.py:36
  289.3 81.3 %all-reduce.20.cloned.1.call-start = ((), (), s32[]{:S(2)}) async-start(), calls=%async_computation.8 | async-start | bytes 131072 | tf_op jit(solution)/shard_map/psum | solution.py:50
Sparse Core Ops, SparseCore 0:
  9.6 17.3 reduce-scatter.1
  45.1 32.1 all-reduce.7
  93.8 31.6 all-reduce.9
  143.3 31.6 all-reduce.11
  191.7 31.6 all-reduce.13
  241.1 31.6 all-reduce.15
  289.4 31.6 all-reduce.17
  338.8 31.6 all-reduce.19
where the time goes:
time: 380 us; the launch traced here: 379 us
  waiting for transfers between devices  239 us (63%)
  blocking collectives  97.8 us (26%)
  matrix products  14.9 us (4%)
  between operations  13.6 us (4%)
  other arithmetic  8.02 us (2%)
  local copies, waits for them, and re-layouts  5.16 us (1%)
    psum x4, waiting for transfers between devices, body(): solved_own = lax.psum(partial_solved, 'col')  128 us
    psum x3, waiting for transfers between devices, body(): summed = lax.psum(accumulated[first_row:last_row], 'col')  95.3 us
    all_gather x4, blocking collectives, body(): lax.all_gather(target_rows[:, None], 'row', axis=1, tiled=True)  55.5 us
    all_gather x3, blocking collectives, body(): lax.all_gather(solved_own[:, None], 'row', axis=1, tiled=True)  42.3 us
    reduce_scatter x1, waiting for transfers between devices, body(): lax.psum_scatter(below[0, :, 0], 'layer', scatter_dimension=1, tiled=True)  16.2 us
    dot_general x4, matrix products, body(): jnp.einsum('exnc,xvc->evn', inverted_diagonal[current_supernode], local_t...  11.6 us
  transfers between devices with their start and end apart: 8, of which 8 were waited for; matrix products, arithmetic and copies ran while one was open for 1% of the time, Pallas kernels for 0%

commit v1 on v0

--- a/solution.py
+++ b/solution.py
@@ -33,7 +33,9 @@
         merged_part = merged[first_row:last_row]
         offset = col_index - current_supernode * NB
         active = ((offset >= 0) & (offset < NB)).astype(jnp.float32)
-        summed = lax.psum(accumulated[first_row:last_row], "col")
+        block = accumulated[first_row:last_row]
+        parts = lax.all_gather(block, "col", axis=0, tiled=False)
+        summed = parts.sum(axis=0)
         target_rows = merged_part - summed
         relayed = lax.all_gather(target_rows[:, None], "row", axis=1, tiled=True).reshape(
             NB, rhs_width, BLK

time: 380 us -> 299 us (0.79)
  waiting for transfers between devices: 239 us -> 146 us
  blocking collectives: 97.8 us -> 115 us
    psum x3 -> x0, waiting for transfers between devices: 95.3 us -> none  [body(): summed = lax.psum(accumulated[first_row:last_row], 'col')]
    all_gather x0 -> x3, blocking collectives: none -> 17.3 us  [body(): parts = lax.all_gather(block, 'col', axis=0, tiled=False)]
  transfers between devices with their start and end apart: 8 -> 5, of which waited for: 8 -> 5; matrix products, arithmetic and copies ran while one was open for 1% -> 1% of each run, Pallas kernels for 0% -> 0%
where the time goes in v1:
time: 299 us; the launch traced here: 298 us
  waiting for transfers between devices  146 us (49%)
  blocking collectives  115 us (38%)
  matrix products  14.9 us (5%)
  between operations  13.3 us (4%)
  other arithmetic  5.04 us (2%)
  local copies, waits for them, and re-layouts  3.93 us (1%)
    psum x4, waiting for transfers between devices, body(): solved_own = lax.psum(partial_solved, 'col')  129 us
    all_gather x4, blocking collectives, body(): lax.all_gather(target_rows[:, None], 'row', axis=1, tiled=True)  55.5 us
    all_gather x3, blocking collectives, body(): lax.all_gather(solved_own[:, None], 'row', axis=1, tiled=True)  42.3 us
    all_gather x3, blocking collectives, body(): parts = lax.all_gather(block, 'col', axis=0, tiled=False)  17.3 us
    reduce_scatter x1, waiting for transfers between devices, body(): lax.psum_scatter(below[0, :, 0], 'layer', scatter_dimension=1, tiled=True)  16.2 us
    dot_general x4, matrix products, body(): jnp.einsum('exnc,xvc->evn', inverted_diagonal[current_supernode], local_t...  11.6 us
  transfers between devices with their start and end apart: 5, of which 5 were waited for; matrix products, arithmetic and copies ran while one was open for 1% of the time, Pallas kernels for 0%

profile of v1, /device:TPU:0, one launch (start us, length us, event | category | flops | bytes accessed | tf_op | source)
XLA Modules:
  0.0 298.2 jit_solution(11721482311236933981)
XLA Ops:
  6.5 2.2 copy.83
  8.8 0.7 and_select_fusion
  10.1 0.7 compare_and_fusion
  10.8 16.2 %reduce-scatter.2.cloned.1.call-done = f32[16,32,128]{2,0,1:T(8,128)} async-done(((f32[16,64,128]{2,0,1:T(8,128)}), f32[16,32,128]{2,0,1:T(8,128)}) %reduce-scatter.2.cloned.1.call-update) | async-done | bytes 262160 | tf_op jit(solution)/shard_map/reduce_scatter | solution.py:27
  27.0 1.2 bitcast_subtract_fusion
  28.2 13.9 %all-gather = f32[4,128,128]{2,0,1:T(4,128)S(1)} all-gather(f32[4,32,128]{2,0,1:T(4,128)S(1)} %slice.54), channel_id=2, replica_groups=mesh['layer'=2,'row'=4,'col'=4] {'row'}, dimensions={1}, use_global_device_ids=true | all-gather | bytes 327680 | tf_op jit(solution)/shard_map/all_gather | solution.py:40
  42.1 2.9 convolution_bitcast_fusion.3
  45.1 32.2 %all-reduce.5.cloned.1.call-done = f32[4,32,128]{2,1,0:T(8,128)} async-done(((f32[4,32,128]{2,1,0:T(8,128)}), f32[4,32,128]{2,1,0:T(8,128)}) %all-reduce.5.cloned.1.call-update) | async-done | bytes 65552 | tf_op jit(solution)/shard_map/psum | solution.py:52
  77.3 14.1 %all-gather.1 = f32[4,128,128]{2,1,0:T(8,128)S(1)} all-gather(f32[4,32,128]{2,1,0:T(8,128)} %all-reduce.5.cloned.1.call-done), channel_id=3, replica_groups=mesh['layer'=2,'row'=4,'col'=4] {'row'}, dimensions={1}, use_global_device_ids=true | all-gather | bytes 327680 | tf_op jit(solution)/shard_map/all_gather | solution.py:54
  93.1 5.8 %all-gather.2 = f32[16,32,128]{2,1,0:T(8,128)S(1)} all-gather(f32[4,32,128]{2,1,0:T(8,128)S(1)} %copy.38), channel_id=4, replica_groups=mesh['layer'=2,'row'=4,'col'=4] {'col'}, dimensions={0}, use_global_device_ids=true | all-gather | bytes 327680 | tf_op jit(solution)/shard_map/all_gather | solution.py:37
  98.9 13.9 %all-gather.3 = f32[4,128,128]{2,0,1:T(4,128)S(1)} all-gather(f32[4,32,128]{2,0,1:T(4,128)S(1)} %slice_subtract_fusion.2), channel_id=5, replica_groups=mesh['layer'=2,'row'=4,'col'=4] {'row'}, dimensions={1}, use_global_device_ids=true | all-gather | bytes 327680 | tf_op jit(solution)/shard_map/all_gather | solution.py:40
  112.8 2.9 convolution_bitcast_fusion.2
  115.8 32.4 %all-reduce.7.cloned.1.call-done = f32[4,32,128]{2,1,0:T(8,128)} async-done(((f32[4,32,128]{2,1,0:T(8,128)}), f32[4,32,128]{2,1,0:T(8,128)}) %all-reduce.7.cloned.1.call-update) | async-done | bytes 65552 | tf_op jit(solution)/shard_map/psum | solution.py:52
  148.2 14.2 %all-gather.4 = f32[4,128,128]{2,1,0:T(8,128)S(1)} all-gather(f32[4,32,128]{2,1,0:T(8,128)} %all-reduce.7.cloned.1.call-done), channel_id=6, replica_groups=mesh['layer'=2,'row'=4,'col'=4] {'row'}, dimensions={1}, use_global_device_ids=true | all-gather | bytes 327680 | tf_op jit(solution)/shard_map/all_gather | solution.py:54
  164.1 5.8 %all-gather.5 = f32[16,32,128]{2,1,0:T(8,128)S(1)} all-gather(f32[4,32,128]{2,1,0:T(8,128)S(1)} %copy.43), channel_id=7, replica_groups=mesh['layer'=2,'row'=4,'col'=4] {'col'}, dimensions={0}, use_global_device_ids=true | all-gather | bytes 327680 | tf_op jit(solution)/shard_map/all_gather | solution.py:37
  169.9 13.9 %all-gather.6 = f32[4,128,128]{2,0,1:T(4,128)S(1)} all-gather(f32[4,32,128]{2,0,1:T(4,128)S(1)} %slice_subtract_fusion.1), channel_id=8, replica_groups=mesh['layer'=2,'row'=4,'col'=4] {'row'}, dimensions={1}, use_global_device_ids=true | all-gather | bytes 327680 | tf_op jit(solution)/shard_map/all_gather | solution.py:40
  183.8 2.9 convolution_bitcast_fusion.1
  186.8 32.4 %all-reduce.9.cloned.1.call-done = f32[4,32,128]{2,1,0:T(8,128)} async-done(((f32[4,32,128]{2,1,0:T(8,128)}), f32[4,32,128]{2,1,0:T(8,128)}) %all-reduce.9.cloned.1.call-update) | async-done | bytes 65552 | tf_op jit(solution)/shard_map/psum | solution.py:52
  219.2 14.1 %all-gather.7 = f32[4,128,128]{2,1,0:T(8,128)S(1)} all-gather(f32[4,32,128]{2,1,0:T(8,128)} %all-reduce.9.cloned.1.call-done), channel_id=9, replica_groups=mesh['layer'=2,'row'=4,'col'=4] {'row'}, dimensions={1}, use_global_device_ids=true | all-gather | bytes 327680 | tf_op jit(solution)/shard_map/all_gather | solution.py:54
  235.0 5.8 %all-gather.8 = f32[16,32,128]{2,1,0:T(8,128)S(1)} all-gather(f32[4,32,128]{2,1,0:T(8,128)S(1)} %copy.48), channel_id=10, replica_groups=mesh['layer'=2,'row'=4,'col'=4] {'col'}, dimensions={0}, use_global_device_ids=true | all-gather | bytes 327680 | tf_op jit(solution)/shard_map/all_gather | solution.py:37
  240.8 13.9 %all-gather.9 = f32[4,128,128]{2,0,1:T(4,128)S(1)} all-gather(f32[4,32,128]{2,0,1:T(4,128)S(1)} %slice_subtract_fusion), channel_id=11, replica_groups=mesh['layer'=2,'row'=4,'col'=4] {'row'}, dimensions={1}, use_global_device_ids=true | all-gather | bytes 327680 | tf_op jit(solution)/shard_map/all_gather | solution.py:40
  254.7 2.9 convolution_bitcast_fusion
  257.6 32.4 %all-reduce.11.cloned.1.call-done = f32[4,32,128]{2,1,0:T(8,128)} async-done(((f32[4,32,128]{2,1,0:T(8,128)}), f32[4,32,128]{2,1,0:T(8,128)}) %all-reduce.11.cloned.1.call-update) | async-done | bytes 65552 | tf_op jit(solution)/shard_map/psum | solution.py:52
  290.0 1.6 maximum_bitcast_fusion
  (46 shorter events, 6.2 us)
Async XLA Ops:
  6.5 85.4 %copy-start = (f32[1,1,4,128,128]{4,3,2,1,0:T(8,128)S(1)}, f32[1,1,4,128,128]{4,3,2,1,0:T(8,128)}, u32[]{:S(2)}) copy-start(f32[1,1,4,128,128]{4,3,2,1,0:T(8,128)} %param.11) | copy-start | bytes 786436
  6.5 20.4 %reduce-scatter.2.cloned.1.call-start = ((), (), s32[]{:S(2)}) async-start(), calls=%async_computation.1 | async-start | bytes 786432 | tf_op jit(solution)/shard_map/reduce_scatter | solution.py:27
  8.7 68.6 %all-reduce.5.cloned.1.call-start = ((), (), s32[]{:S(2)}) async-start(), calls=%async_computation.2 | async-start | bytes 131072 | tf_op jit(solution)/shard_map/psum | solution.py:52
  45.0 103.2 %all-reduce.7.cloned.1.call-start = ((), (), s32[]{:S(2)}) async-start(), calls=%async_computation.3 | async-start | bytes 131072 | tf_op jit(solution)/shard_map/psum | solution.py:52
  115.7 174.3 %copy-start.1 = (f32[4,32,128]{2,1,0:T(8,128)S(1)}, f32[4,32,128]{2,1,0:T(8,128)}, u32[]{:S(2)}) copy-start(f32[4,32,128]{2,1,0:T(8,128)} %all-reduce.5.cloned.1.call-done) | copy-start | bytes 196612
  115.8 103.4 %all-reduce.9.cloned.1.call-start = ((), (), s32[]{:S(2)}) async-start(), calls=%async_computation.4 | async-start | bytes 131072 | tf_op jit(solution)/shard_map/psum | solution.py:52
  148.2 141.9 %copy-start.2 = (f32[4,32,128]{2,1,0:T(8,128)S(1)}, f32[4,32,128]{2,1,0:T(8,128)}, u32[]{:S(2)}) copy-start(f32[4,32,128]{2,1,0:T(8,128)} %all-reduce.7.cloned.1.call-done) | copy-start | bytes 196612
  186.7 103.3 %all-reduce.11.cloned.1.call-start = ((), (), s32[]{:S(2)}) async-start(), calls=%async_computation.5 | async-start | bytes 131072 | tf_op jit(solution)/shard_map/psum | solution.py:52
Sparse Core Ops, SparseCore 0:
  9.6 17.3 reduce-scatter.1
  45.1 32.1 all-reduce.4
  115.9 32.2 all-reduce.6
  186.9 32.2 all-reduce.8
  257.7 32.2 all-reduce.10
